TPU v7x, 32 devices: a whole 2x2x4 slice. The times are simulated.
32 devices in a mesh: dp: 8 (over z, x), tensor: 4 (over y, core).
Axes of the slice: x: 2, y: 2, z: 4, core: 2. Of those that a mesh axis runs over, the one named last changes fastest.
Arguments:
- layer_input: bfloat16 [8192, 512], P(('dp', 'tensor')), may hold values from -6 to 6
- segments: int32 [8, 1024], P('dp'), may hold values from 0 to 3, never falling along the last dimension, each value on 1 to 800 neighbouring positions
- norm1_gain: bfloat16 [512], replicated, may hold values from 0.5 to 1.5
- norm1_bias: bfloat16 [512], replicated, may hold values from -4 to 4
- w_query: bfloat16 [512, 512], P(None, 'tensor'), may hold values from -0.25 to 0.25
- b_query: bfloat16 [512], P('tensor'), may hold values from -6 to 6
- w_key: bfloat16 [512, 512], P(None, 'tensor'), may hold values from -0.25 to 0.25
- w_value: bfloat16 [512, 512], P(None, 'tensor'), may hold values from -0.25 to 0.25
- b_value: bfloat16 [512], P('tensor'), may hold values from -6 to 6
- w_out: bfloat16 [512, 512], P('tensor'), may hold values from -2 to 2
- b_out: bfloat16 [512], replicated, may hold values from -4 to 4
- gate1_w: bfloat16 [512, 512], P('tensor'), may hold values from -0.25 to 0.25
- gate1_b: bfloat16 [512], replicated, may hold values from -6 to 6
- norm2_gain: bfloat16 [512], replicated, may hold values from 0.5 to 1.5
- norm2_bias: bfloat16 [512], replicated, may hold values from -4 to 4
- w_in: bfloat16 [512, 2048], P(None, 'tensor'), may hold values from -0.25 to 0.25
- b_in: bfloat16 [2048], P('tensor'), may hold values from -6 to 6
- w_back: bfloat16 [2048, 512], P('tensor'), may hold values from -0.1875 to 0.1875
- b_back: bfloat16 [512], replicated, may hold values from -4 to 4
- gate2_w: bfloat16 [512, 512], P('tensor'), may hold values from -0.25 to 0.25
- gate2_b: bfloat16 [512], replicated, may hold values from -6 to 6
- cotangent: bfloat16 [8192, 512], P(('dp', 'tensor')), may hold values from -6 to 6
Outputs:
- output: bfloat16 [8192, 512], P(('dp', 'tensor'))
- input_grad: float32 [8192, 512], P(('dp', 'tensor'))
- grad_norm1_gain: float32 [512], replicated
- grad_norm1_bias: float32 [512], replicated
- grad_w_query: float32 [512, 512], P(None, 'tensor')
- grad_b_query: float32 [512], P('tensor')
- grad_w_key: float32 [512, 512], P(None, 'tensor')
- grad_w_value: float32 [512, 512], P(None, 'tensor')
- grad_b_value: float32 [512], P('tensor')
- grad_w_out: float32 [512, 512], P('tensor')
- grad_b_out: float32 [512], replicated
- grad_gate1_w: float32 [512, 512], P('tensor')
- grad_gate1_b: float32 [512], replicated
- grad_norm2_gain: float32 [512], replicated
- grad_norm2_bias: float32 [512], replicated
- grad_w_in: float32 [512, 2048], P(None, 'tensor')
- grad_b_in: float32 [2048], P('tensor')
- grad_w_back: float32 [2048, 512], P('tensor')
- grad_b_back: float32 [512], replicated
- grad_gate2_w: float32 [512, 512], P('tensor')
- grad_gate2_b: float32 [512], replicated
Inputs may be any that keep to these rules, and one draw needn't show every extreme that they name: `segments`: document numbers never fall along a sequence; every sequence holds 4 documents, none longer than 800 tokens, and one document reaches that length.
All inputs are finite; a program needn't handle non-finite values.
Results may differ from a plain program's by a relative error of at most 0.014.
Values may be sent and summed in bfloat16 or wider, within the bound.
No kernel may reach another device: no remote copies, remote signals or barrier semaphores. Data moves between devices by JAX's collectives and lax.ppermute only.
A program may use at most 64 MiB of HBM per device.

v0:
```python
import jax
import jax.numpy as jnp
from jax import lax
from jax.sharding import PartitionSpec as P

HD = 64
EPSILON = 1e-05


def matmul(left, right):
    return jnp.dot(left, right, preferred_element_type=jnp.float32)


def inner_left(left, right):
    return lax.dot_general(
        left, right, (((0,), (0,)), ((), ())), preferred_element_type=jnp.float32
    )


def outer_right(left, right):
    return lax.dot_general(
        left, right, (((1,), (1,)), ((), ())), preferred_element_type=jnp.float32
    )


def column_sum(matrix):
    return jnp.sum(matrix, axis=0, dtype=jnp.float32)


def place_columns(full, piece, start):
    current = lax.dynamic_slice_in_dim(full, start, piece.shape[1], 1)
    return lax.dynamic_update_slice_in_dim(full, current + piece, start, 1)


def smooth_unit(values):
    return jax.nn.gelu(values, approximate=True)


def norm_forward(values, gain, shift):
    centred = values - jnp.mean(values, axis=-1, keepdims=True)
    spread = jnp.mean(centred * centred, axis=-1, keepdims=True)
    inverse = lax.rsqrt(spread + EPSILON)
    unit = centred * inverse
    return (unit * gain + shift, unit, inverse)


def norm_backward(share_grad, unit, inverse, gain):
    scaled = share_grad * gain
    grad_gain = jnp.sum(share_grad * unit, axis=0)
    grad_shift = jnp.sum(share_grad, axis=0)
    average = jnp.mean(scaled, axis=-1, keepdims=True)
    project = jnp.mean(scaled * unit, axis=-1, keepdims=True)
    return (inverse * (scaled - average - unit * project), grad_gain, grad_shift)


def head_major(matrix):
    return matrix.reshape(matrix.shape[0], -1, HD).transpose(1, 0, 2)


def row_major(heads_array):
    return heads_array.transpose(1, 0, 2).reshape(heads_array.shape[1], -1)


def split_blocks(heads_array, count, block):
    return heads_array.reshape(heads_array.shape[0], count, block, HD).transpose(1, 0, 2, 3)


def join_blocks(blocks):
    count, heads, block, width = blocks.shape
    return blocks.transpose(0, 2, 1, 3).reshape(count * block, heads * width)


def build_mask(segment_row):
    places = lax.iota(jnp.int32, segment_row.shape[0])
    same_doc = segment_row[:, None] == segment_row[None, :]
    return same_doc & (places[None, :] <= places[:, None])


def attention_forward(query, keys, values, allowed):
    rows = query.shape[0]
    block = min(512, rows)
    count = rows // block
    scale_factor = HD ** (-0.5)
    heads_k = head_major(keys)
    heads_v = head_major(values)
    query_blocks = split_blocks(head_major(query), count, block)
    mask_blocks = allowed.reshape(count, block, rows)

    def one_block(pieces):
        query_block, mask_block = pieces
        scores = (
            jnp.einsum("hqd,hkd->hqk", query_block, heads_k, preferred_element_type=jnp.float32)
            * scale_factor
        )
        scores = jnp.where(mask_block[None], scores, -1e30)
        totals = jax.nn.logsumexp(scores, axis=-1, keepdims=True)
        probs = jnp.exp(scores - totals).astype(jnp.bfloat16)
        mixed = jnp.einsum("hqk,hkd->hqd", probs, heads_v, preferred_element_type=jnp.float32)
        return (mixed, totals)

    mixed, totals = lax.map(one_block, (query_blocks, mask_blocks))
    return (join_blocks(mixed).astype(jnp.bfloat16), totals)


def attention_backward(query, keys, values, allowed, totals, attended_grad):
    rows = query.shape[0]
    block = min(512, rows)
    count = rows // block
    scale_factor = HD ** (-0.5)
    heads_k = head_major(keys)
    heads_v = head_major(values)
    query_blocks = split_blocks(head_major(query), count, block)
    grad_blocks = split_blocks(head_major(attended_grad), count, block)
    mask_blocks = allowed.reshape(count, block, rows)

    def one_block(carry, pieces):
        key_acc, value_acc = carry
        query_block, grad_block, mask_block, total_block = pieces
        scores = (
            jnp.einsum("hqd,hkd->hqk", query_block, heads_k, preferred_element_type=jnp.float32)
            * scale_factor
        )
        scores = jnp.where(mask_block[None], scores, -1e30)
        probs = jnp.exp(scores - total_block)
        prob_low = probs.astype(jnp.bfloat16)
        prob_grad = jnp.einsum(
            "hqd,hkd->hqk", grad_block, heads_v, preferred_element_type=jnp.float32
        )
        weighted = jnp.sum(probs * prob_grad, axis=-1, keepdims=True)
        score_grad = (probs * (prob_grad - weighted)).astype(jnp.bfloat16)
        query_part = (
            jnp.einsum("hqk,hkd->hqd", score_grad, heads_k, preferred_element_type=jnp.float32)
            * scale_factor
        )
        key_acc = (
            key_acc
            + jnp.einsum(
                "hqk,hqd->hkd", score_grad, query_block, preferred_element_type=jnp.float32
            )
            * scale_factor
        )
        value_acc = value_acc + jnp.einsum(
            "hqk,hqd->hkd", prob_low, grad_block, preferred_element_type=jnp.float32
        )
        return ((key_acc, value_acc), query_part.astype(jnp.bfloat16))

    empty = jnp.zeros(heads_k.shape, jnp.float32)
    (key_acc, value_acc), query_parts = lax.scan(
        one_block, (empty, empty), (query_blocks, grad_blocks, mask_blocks, totals)
    )
    return (
        join_blocks(query_parts),
        row_major(key_acc).astype(jnp.bfloat16),
        row_major(value_acc).astype(jnp.bfloat16),
    )


def forward_pass(layer_input, segments, weights):
    (
        norm1_gain,
        norm1_bias,
        w_query,
        b_query,
        w_key,
        w_value,
        b_value,
        w_out,
        b_out,
        gate1_w,
        gate1_b,
        norm2_gain,
        norm2_bias,
        w_in,
        b_in,
        w_back,
        b_back,
        gate2_w,
        gate2_b,
    ) = weights
    start_col = lax.axis_index("tensor") * gate1_w.shape[0]
    inputs = layer_input.astype(jnp.float32)
    normed_part, unit_one, inverse_one = norm_forward(
        inputs, norm1_gain.astype(jnp.float32), norm1_bias.astype(jnp.float32)
    )
    normed_low = normed_part.astype(jnp.bfloat16)
    normed = lax.all_gather(normed_low, "tensor", axis=0, tiled=True)
    query = (matmul(normed, w_query) + b_query.astype(jnp.float32)).astype(jnp.bfloat16)
    keys = matmul(normed, w_key).astype(jnp.bfloat16)
    values = (matmul(normed, w_value) + b_value.astype(jnp.float32)).astype(jnp.bfloat16)
    allowed = build_mask(segments[0])
    attended, totals = attention_forward(query, keys, values, allowed)
    gate_rows = lax.dynamic_slice_in_dim(normed, start_col, gate1_w.shape[0], 1)
    branch_part, logit_one = (
        lax.psum_scatter(matmul(attended, w_out), "tensor", scatter_dimension=0, tiled=True),
        lax.psum_scatter(matmul(gate_rows, gate1_w), "tensor", scatter_dimension=0, tiled=True),
    )
    branch = branch_part + b_out.astype(jnp.float32)
    gate_one = jax.nn.sigmoid(logit_one + gate1_b.astype(jnp.float32))
    middle = inputs + gate_one * branch
    normed_two_part, unit_two, inverse_two = norm_forward(
        middle, norm2_gain.astype(jnp.float32), norm2_bias.astype(jnp.float32)
    )
    normed_two = lax.all_gather(normed_two_part.astype(jnp.bfloat16), "tensor", axis=0, tiled=True)
    hidden_input = matmul(normed_two, w_in) + b_in.astype(jnp.float32)
    hidden = smooth_unit(hidden_input).astype(jnp.bfloat16)
    gate_rows_two = lax.dynamic_slice_in_dim(normed_two, start_col, gate2_w.shape[0], 1)
    ffn_part, logit_two = (
        lax.psum_scatter(matmul(hidden, w_back), "tensor", scatter_dimension=0, tiled=True),
        lax.psum_scatter(matmul(gate_rows_two, gate2_w), "tensor", scatter_dimension=0, tiled=True),
    )
    ffn_out = ffn_part + b_back.astype(jnp.float32)
    gate_two = jax.nn.sigmoid(logit_two + gate2_b.astype(jnp.float32))
    result = middle + gate_two * ffn_out
    saved = (
        normed,
        normed_low,
        query,
        keys,
        values,
        allowed,
        attended,
        totals,
        branch,
        gate_one,
        unit_one,
        inverse_one,
        normed_two,
        hidden,
        hidden_input,
        ffn_out,
        gate_two,
        unit_two,
        inverse_two,
    )
    return (result, saved)


def body(
    layer_input,
    segments,
    norm1_gain,
    norm1_bias,
    w_query,
    b_query,
    w_key,
    w_value,
    b_value,
    w_out,
    b_out,
    gate1_w,
    gate1_b,
    norm2_gain,
    norm2_bias,
    w_in,
    b_in,
    w_back,
    b_back,
    gate2_w,
    gate2_b,
    cotangent,
):
    weights = (
        norm1_gain,
        norm1_bias,
        w_query,
        b_query,
        w_key,
        w_value,
        b_value,
        w_out,
        b_out,
        gate1_w,
        gate1_b,
        norm2_gain,
        norm2_bias,
        w_in,
        b_in,
        w_back,
        b_back,
        gate2_w,
        gate2_b,
    )
    result, saved = forward_pass(layer_input, segments, weights)
    barrier = lax.optimization_barrier((layer_input, weights))
    unused, saved = forward_pass(barrier[0], segments, barrier[1])
    (
        normed,
        normed_low,
        query,
        keys,
        values,
        allowed,
        attended,
        totals,
        branch,
        gate_one,
        unit_one,
        inverse_one,
        normed_two,
        hidden,
        hidden_input,
        ffn_out,
        gate_two,
        unit_two,
        inverse_two,
    ) = saved
    start_col = lax.axis_index("tensor") * gate1_w.shape[0]
    upstream = cotangent.astype(jnp.float32)
    ffn_grad = (gate_two * upstream).astype(jnp.bfloat16)
    logit_two_grad = (upstream * ffn_out * (gate_two * (1.0 - gate_two))).astype(jnp.bfloat16)
    ffn_grad_all, logit_two_all = (
        lax.all_gather(ffn_grad, "tensor", axis=0, tiled=True),
        lax.all_gather(logit_two_grad, "tensor", axis=0, tiled=True),
    )
    grad_b_back = column_sum(ffn_grad_all)
    grad_gate2_b = column_sum(logit_two_all)
    grad_w_back = inner_left(hidden, ffn_grad_all)
    unused_value, smooth_pull = jax.vjp(smooth_unit, hidden_input)
    hidden_grad = smooth_pull(outer_right(ffn_grad_all, w_back))[0].astype(jnp.bfloat16)
    grad_w_in = inner_left(normed_two, hidden_grad)
    grad_b_in = column_sum(hidden_grad)
    rows_two = lax.dynamic_slice_in_dim(normed_two, start_col, gate2_w.shape[0], 1)
    grad_gate2_w = inner_left(rows_two, logit_two_all)
    normed_two_grad = place_columns(
        outer_right(hidden_grad, w_in), outer_right(logit_two_all, gate2_w), start_col
    )
    normed_two_share = lax.psum_scatter(normed_two_grad, "tensor", scatter_dimension=0, tiled=True)
    middle_back, grad_norm2_gain, grad_norm2_bias = norm_backward(
        normed_two_share, unit_two, inverse_two, norm2_gain.astype(jnp.float32)
    )
    middle_grad = upstream + middle_back
    ffn_grads = (grad_w_in, grad_b_in, grad_w_back, grad_b_back, grad_gate2_w, grad_gate2_b)
    branch_grad = (gate_one * middle_grad).astype(jnp.bfloat16)
    logit_one_grad = (middle_grad * branch * (gate_one * (1.0 - gate_one))).astype(jnp.bfloat16)
    grad_b_out = column_sum(branch_grad)
    grad_gate1_b = column_sum(logit_one_grad)
    branch_all, logit_one_all = (
        lax.all_gather(branch_grad, "tensor", axis=0, tiled=True),
        lax.all_gather(logit_one_grad, "tensor", axis=0, tiled=True),
    )
    grad_w_out = inner_left(attended, branch_all)
    attended_grad = outer_right(branch_all, w_out).astype(jnp.bfloat16)
    rows_one = lax.dynamic_slice_in_dim(normed, start_col, gate1_w.shape[0], 1)
    grad_gate1_w = inner_left(rows_one, logit_one_all)
    query_grad, keys_grad, values_grad = attention_backward(
        query, keys, values, allowed, totals, attended_grad
    )
    grad_w_query = inner_left(normed, query_grad)
    grad_b_query = column_sum(query_grad)
    grad_w_key = inner_left(normed, keys_grad)
    grad_w_value = inner_left(normed, values_grad)
    grad_b_value = column_sum(values_grad)
    normed_grad = (
        outer_right(query_grad, w_query)
        + outer_right(keys_grad, w_key)
        + outer_right(values_grad, w_value)
    )
    normed_grad = place_columns(normed_grad, outer_right(logit_one_all, gate1_w), start_col)
    normed_share = lax.psum_scatter(
        normed_grad.astype(jnp.bfloat16), "tensor", scatter_dimension=0, tiled=True
    ).astype(jnp.float32)
    input_back, grad_norm1_gain, grad_norm1_bias = norm_backward(
        normed_share, unit_one, inverse_one, norm1_gain.astype(jnp.float32)
    )
    input_grad = middle_grad + input_back
    norm_sums = lax.psum(
        (
            grad_norm1_gain,
            grad_norm1_bias,
            grad_norm2_gain,
            grad_norm2_bias,
            grad_b_out,
            grad_gate1_b,
        ),
        ("dp", "tensor"),
    )
    attention_grads = (
        grad_w_query,
        grad_b_query,
        grad_w_key,
        grad_w_value,
        grad_b_value,
        grad_w_out,
        grad_gate1_w,
    )
    every_grad = lax.psum(
        (
            grad_w_query,
            grad_b_query,
            grad_w_key,
            grad_w_value,
            grad_b_value,
            grad_w_out,
            grad_gate1_w,
            grad_w_in,
            grad_b_in,
            grad_w_back,
            grad_b_back,
            grad_gate2_w,
            grad_gate2_b,
        ),
        "dp",
    )
    attention_grads = every_grad[0:7]
    ffn_grads = every_grad[7:13]
    return (
        result.astype(jnp.bfloat16),
        input_grad,
        norm_sums[0],
        norm_sums[1],
        attention_grads[0],
        attention_grads[1],
        attention_grads[2],
        attention_grads[3],
        attention_grads[4],
        attention_grads[5],
        norm_sums[4],
        attention_grads[6],
        norm_sums[5],
        norm_sums[2],
        norm_sums[3],
        ffn_grads[0],
        ffn_grads[1],
        ffn_grads[2],
        ffn_grads[3],
        ffn_grads[4],
        ffn_grads[5],
    )


def solution(mesh):
    placed = (
        P(("dp", "tensor"), None),
        P("dp", None),
        P(),
        P(),
        P(None, "tensor"),
        P("tensor"),
        P(None, "tensor"),
        P(None, "tensor"),
        P("tensor"),
        P("tensor", None),
        P(),
        P("tensor", None),
        P(),
        P(),
        P(),
        P(None, "tensor"),
        P("tensor"),
        P("tensor", None),
        P(),
        P("tensor", None),
        P(),
        P(("dp", "tensor"), None),
    )
    return jax.shard_map(
        body,
        mesh=mesh,
        in_specs=placed,
        out_specs=(
            P(("dp", "tensor"), None),
            P(("dp", "tensor"), None),
            P(),
            P(),
            P(None, "tensor"),
            P("tensor"),
            P(None, "tensor"),
            P(None, "tensor"),
            P("tensor"),
            P("tensor", None),
            P(),
            P("tensor", None),
            P(),
            P(),
            P(),
            P(None, "tensor"),
            P("tensor"),
            P("tensor", None),
            P(),
            P("tensor", None),
            P(),
        ),
        check_vma=False,
    )
```

profile of v0, /device:TPU:0, one launch (start us, length us, event | category | flops | bytes accessed | tf_op | source)
XLA Modules:
  0.0 718.7 jit_solution(1008536278620861501)
XLA Ops:
  11.0 1.9 fusion.90
  16.1 1.9 fusion.52
  18.0 14.4 %all-gather.13.cloned.1.call-done = bf16[1024,512]{1,0:T(8,128)(2,1)} async-done(((bf16[256,512]{1,0:T(8,128)(2,1)}), bf16[1024,512]{1,0:T(8,128)(2,1)}) %all-gather.13.cloned.1.call-update) | async-done | bytes 1048592 | tf_op jit(solution)/shard_map/all_gather | solution.py:186
  32.5 1.8 fusion.73
  36.2 8.7 %while.38 = (s32[]{:T(128)}, bf16[2,2,512,64]{2,3,1,0:T(8,128)(2,1)}, f32[2,2,512,1]{2,1,3,0:T(2,128)S(1)}, pred[2,512,1024]{2,1,0:T(8,128)(4,1)S(1)}, bf16[2,2,...) while((s32[]{:T(128)}, ...), condition=%wide.region_18.19_spmd, body=%wide.region_15.18_spmd.sunk | while | flops 279977984 | bytes 18268324 | solution.py:101
  46.9 1.8 fusion.133
  48.9 2.7 fusion.116
  54.8 25.5 %reduce-scatter.21.cloned.1.call-done = f32[256,512]{1,0:T(8,128)} async-done(((f32[1024,512]{1,0:T(8,128)}), f32[256,512]{1,0:T(8,128)}) %reduce-scatter.21.cloned.1.call-update) | async-done | bytes 524304 | tf_op jit(solution)/shard_map/reduce_scatter | solution.py:194
  80.3 34.1 %reduce-scatter.19.cloned.1.call-done = f32[256,512]{1,0:T(8,128)} async-done(((f32[1024,512]{1,0:T(8,128)}), f32[256,512]{1,0:T(8,128)}) %reduce-scatter.19.cloned.1.call-update) | async-done | bytes 524304 | tf_op jit(solution)/shard_map/reduce_scatter | solution.py:195
  118.3 16.8 %all-gather.15.cloned.1.call-done = bf16[1024,512]{1,0:T(8,128)(2,1)} async-done(((bf16[256,512]{1,0:T(8,128)(2,1)}), bf16[1024,512]{1,0:T(8,128)(2,1)}) %all-gather.15.cloned.1.call-update) | async-done | bytes 1048592 | tf_op jit(solution)/shard_map/all_gather | solution.py:203
  135.1 2.7 fusion.112
  138.6 30.8 %reduce-scatter.23.cloned.1.call-done = f32[256,512]{1,0:T(8,128)} async-done(((f32[1024,512]{1,0:T(8,128)}), f32[256,512]{1,0:T(8,128)}) %reduce-scatter.23.cloned.1.call-update) | async-done | bytes 524304 | tf_op jit(solution)/shard_map/reduce_scatter | solution.py:209
  169.5 2.0 fusion.100
  172.8 3.4 fusion.134
  176.2 12.2 %all-gather.17.cloned.1.call-done = bf16[1024,512]{1,0:T(8,128)(2,1)} async-done(((bf16[256,512]{1,0:T(8,128)(2,1)}), bf16[1024,512]{1,0:T(8,128)(2,1)}) %all-gather.17.cloned.1.call-update) | async-done | bytes 1048592 | tf_op jit(solution)/shard_map/all_gather | solution.py:312
  188.4 5.5 convert_reduce_fusion.2
  194.8 2.0 fusion.136
  198.2 30.3 %reduce-scatter.25.cloned.1.call-done = f32[256,512]{1,0:T(8,128)} async-done(((f32[1024,512]{1,0:T(8,128)}), f32[256,512]{1,0:T(8,128)}) %reduce-scatter.25.cloned.1.call-update) | async-done | bytes 524304 | tf_op jit(solution)/shard_map/reduce_scatter | solution.py:208
  228.5 2.2 fusion.102
  230.9 3.4 fusion.135
  234.4 13.2 %all-gather.19.cloned.1.call-done = bf16[1024,512]{1,0:T(8,128)(2,1)} async-done(((bf16[256,512]{1,0:T(8,128)(2,1)}), bf16[1024,512]{1,0:T(8,128)(2,1)}) %all-gather.19.cloned.1.call-update) | async-done | bytes 1048592 | tf_op jit(solution)/shard_map/all_gather | solution.py:313
  247.6 2.7 fusion.69
  251.1 30.8 %reduce-scatter.27.cloned.1.call-done = f32[256,512]{1,0:T(8,128)} async-done(((f32[1024,512]{1,0:T(8,128)}), f32[256,512]{1,0:T(8,128)}) %reduce-scatter.27.cloned.1.call-update) | async-done | bytes 524304 | tf_op jit(solution)/shard_map/reduce_scatter | solution.py:327
  281.9 2.1 multiply_reduce_fusion.1
  284.1 3.3 convert_reduce_fusion.6
  289.6 16.1 %all-gather.21.cloned.1.call-done = bf16[1024,512]{1,0:T(8,128)(2,1)} async-done(((bf16[256,512]{1,0:T(8,128)(2,1)}), bf16[1024,512]{1,0:T(8,128)(2,1)}) %all-gather.21.cloned.1.call-update) | async-done | bytes 1048592 | tf_op jit(solution)/shard_map/all_gather | solution.py:338
  305.7 2.4 convolution_convert_fusion
  308.1 1.9 reshape.269
  310.0 1.7 copy.48
  311.7 16.5 %while.39 = (s32[]{:T(128)}, f32[2,1024,64]{1,2,0:T(8,128)}, f32[2,1024,64]{1,2,0:T(8,128)}, bf16[2,2,512,64]{2,3,1,0:T(8,128)(2,1)}, pred[2,512,1024]{2,1,0:T(8...) while((s32[]{:T(128)}, f32[2,1024,64]{1,2,0:T(8,128)}, ...), condition=%wide.region_29.30_spmd.clone, body=%wide.region_27.29_spmd.clone.sunk | while | flops 687602688 | bytes 50229632 | solution.py:148
  314.3 1.8 multiply_reduce_fusion.7
  322.5 1.8 multiply_reduce_fusion.7
  332.4 1.8 add_add_fusion
  334.2 2.7 fusion.68
  336.9 2.7 convert_element_type.273
  343.1 21.6 %reduce-scatter.29.cloned.1.call-done = bf16[256,512]{1,0:T(8,128)(2,1)} async-done(((bf16[1024,512]{1,0:T(8,128)(2,1)}), bf16[256,512]{1,0:T(8,128)(2,1)}) %reduce-scatter.29.cloned.1.call-update) | async-done | bytes 262160 | tf_op jit(solution)/shard_map/reduce_scatter | solution.py:359
  364.7 1.9 fusion.105
  366.6 2.4 fusion.93
  370.4 15.5 %all-gather.9.cloned.1.call-done = bf16[1024,512]{1,0:T(8,128)(2,1)} async-done(((bf16[256,512]{1,0:T(8,128)(2,1)}), bf16[1024,512]{1,0:T(8,128)(2,1)}) %all-gather.9.cloned.1.call-update) | async-done | bytes 1048592 | tf_op jit(solution)/shard_map/all_gather | solution.py:186
  385.9 2.4 fusion.71
  388.3 1.9 reshape.261
  390.2 1.7 copy.43
  391.9 2.7 fusion.108
  394.9 2.4 convolution_convert_fusion.2
  397.3 2.4 fusion.72
  400.4 10.8 %while.37 = (s32[]{:T(128)}, bf16[2,2,512,64]{2,3,1,0:T(8,128)(2,1)}, pred[2,512,1024]{2,1,0:T(8,128)(4,1)S(1)}, bf16[2,2,512,64]{2,3,1,0:T(8,128)(2,1)}, bf16[2...) while((s32[]{:T(128)}, bf16[2,2,512,64]{2,3,1,0:T(8,128)(2,1)}, ...), condition=%wide.region_6.7_spmd, body=%wide.region_3.0_spmd.sunk | while | flops 279973888 | bytes 19304628 | solution.py:101
  400.5 2.1 fusion.236
  405.9 2.1 fusion.236
  412.6 1.8 fusion.132
  414.5 11.7 %reduce-scatter.11.cloned.1.call-done = f32[256,512]{1,0:T(8,128)} async-done(((f32[1024,512]{1,0:T(8,128)}), f32[256,512]{1,0:T(8,128)}) %reduce-scatter.11.cloned.1.call-update) | async-done | bytes 524304 | tf_op jit(solution)/shard_map/reduce_scatter | solution.py:195
  426.2 34.0 %reduce-scatter.13.cloned.1.call-done = f32[256,512]{1,0:T(8,128)} async-done(((f32[1024,512]{1,0:T(8,128)}), f32[256,512]{1,0:T(8,128)}) %reduce-scatter.13.cloned.1.call-update) | async-done | bytes 524304 | tf_op jit(solution)/shard_map/reduce_scatter | solution.py:194
  462.9 16.8 %all-gather.11.cloned.1.call-done = bf16[1024,512]{1,0:T(8,128)(2,1)} async-done(((bf16[256,512]{1,0:T(8,128)(2,1)}), bf16[1024,512]{1,0:T(8,128)(2,1)}) %all-gather.11.cloned.1.call-update) | async-done | bytes 1048592 | tf_op jit(solution)/shard_map/all_gather | solution.py:203
  479.7 4.1 fusion.70
  484.7 2.7 fusion.106
  487.4 3.4 fusion.144
  490.8 1.7 fusion.143
  501.2 22.1 %all-reduce.1 = (f32[128]{0:T(128)}, f32[128]{0:T(128)}, f32[512]{0:T(512)}, f32[512]{0:T(512)}, f32[512]{0:T(512)}) all-reduce(f32[128]{0:T(128)S(1)} %reduce_sum.253, f32[128]{0:T(128)S(1)} %reduce_sum.255, f32[512]{0:T(512)S(1)} %copy-done.71, f32[512]{0:T(512)S(1)} %convert_reduce_fusion.1, ...), channel_id=1, replica_groups=mesh['dp'=8,'tensor'=4] {'dp'}, use_global_device_ids=true, to_apply=%region_39.40 | all-reduce | flops 1792 | bytes 14336 | tf_op jit(solution)/shard_map/psum | solution.py:386
  523.4 37.1 %all-reduce = (f32[512]{0:T(512)}, f32[512]{0:T(512)}, f32[512]{0:T(512)}, f32[512]{0:T(512)}, f32[512]{0:T(512)}, /*index=5*/f32[512]{0:T(512)}) all-reduce(f32[512]{0:T(512)S(1)} %copy-done.62, f32[512]{0:T(512)S(1)} %copy-done.63, f32[512]{0:T(512)S(1)} %copy-done.61, ...), channel_id=1, replica_groups=mesh['dp'=8,'tensor'=4] {'dp','tensor'}, use_global_device_ids=true, to_apply=%region_34.35 | all-reduce | flops 3072 | bytes 24576 | tf_op jit(solution)/shard_map/psum | solution.py:366
  560.4 2.2 add_convert_fusion.1
  562.6 139.3 %all-reduce.5.cloned.1.call-done = (f32[512,128]{1,0:T(8,128)}, f32[512,128]{1,0:T(8,128)}, f32[512,128]{1,0:T(8,128)}, f32[128,512]{1,0:T(8,128)}, f32[128,512]...) async-done(((f32[512,128]{1,0:T(8,128)}, f32[512,128]{1,0:T(8,128)}, f32[512,128]{1,0:T(8,128)}, f32[128,512]{1,0:T(8,128)}, ...) | async-done | bytes 3670032 | tf_op jit(solution)/shard_map/psum | solution.py:386
  701.9 1.8 copy.96
  703.7 1.8 copy.97
  705.4 1.7 copy.98
  707.1 1.7 copy.99
  (334 shorter events, 80.2 us)
Async XLA Ops:
  7.2 181.2 %copy-start = (bf16[512,512]{1,0:T(8,128)(2,1)S(1)}, bf16[512,512]{1,0:T(8,128)(2,1)}, u32[]{:S(2)}) copy-start(bf16[512,512]{1,0:T(8,128)(2,1)} %param.45) | copy-start | bytes 1572868
  7.2 25.2 %copy-start.23 = (bf16[512,128]{1,0:T(8,128)(2,1)S(1)}, bf16[512,128]{1,0:T(8,128)(2,1)}, u32[]{:S(2)}) copy-start(bf16[512,128]{1,0:T(8,128)(2,1)} %param.32) | copy-start | bytes 393220
  7.2 25.2 %all-gather.13.cloned.1.call-start = ((), (), s32[]{:S(2)}) async-start(), calls=%async_computation.16 | async-start | bytes 1310720 | tf_op jit(solution)/shard_map/all_gather | solution.py:186
  8.4 25.8 %copy-start.48 = (f32[256]{0:T(256)}, f32[256]{0:T(256)S(1)}, u32[]{:S(2)}) copy-start(f32[256]{0:T(256)S(1)} %broadcast_multiply_fusion.5) | copy-start | bytes 3076
  9.6 24.7 %copy-start.52 = (f32[256]{0:T(256)}, f32[256]{0:T(256)S(1)}, u32[]{:S(2)}) copy-start(f32[256]{0:T(256)S(1)} %add_rsqrt_fusion.1) | copy-start | bytes 3076
  11.0 23.5 %copy-start.25 = (bf16[512,128]{1,0:T(8,128)(2,1)S(1)}, bf16[512,128]{1,0:T(8,128)(2,1)}, u32[]{:S(2)}) copy-start(bf16[512,128]{1,0:T(8,128)(2,1)} %param.34) | copy-start | bytes 393220
  12.9 67.5 %reduce-scatter.21.cloned.1.call-start = ((), (), s32[]{:S(2)}) async-start(), calls=%async_computation.18 | async-start | bytes 2621440 | tf_op jit(solution)/shard_map/reduce_scatter | solution.py:194
  18.0 17.0 %copy-start.27 = (bf16[512,128]{1,0:T(8,128)(2,1)S(1)}, bf16[512,128]{1,0:T(8,128)(2,1)}, u32[]{:S(2)}) copy-start(bf16[512,128]{1,0:T(8,128)(2,1)} %param.35) | copy-start | bytes 393220
  32.4 2.1 copy-start.1
  36.2 10.7 %copy-start.22 = (bf16[128,512]{1,0:T(8,128)(2,1)S(1)}, bf16[128,512]{1,0:T(8,128)(2,1)}, u32[]{:S(2)}) copy-start(bf16[128,512]{1,0:T(8,128)(2,1)} %param.37) | copy-start | bytes 393220
  44.9 3.9 copy-start.6
  48.8 65.7 %reduce-scatter.19.cloned.1.call-start = ((), (), s32[]{:S(2)}) async-start(), calls=%async_computation.17 | async-start | bytes 2621440 | tf_op jit(solution)/shard_map/reduce_scatter | solution.py:195
  48.8 2.8 copy-start.65
  48.8 65.6 %copy-start.2 = (bf16[256,512]{1,0:T(8,128)(2,1)S(1)}, bf16[256,512]{1,0:T(8,128)(2,1)}, u32[]{:S(2)}) copy-start(bf16[256,512]{1,0:T(8,128)(2,1)} %param.28) | copy-start | bytes 786436
  51.6 83.6 %all-gather.15.cloned.1.call-start = ((), (), s32[]{:S(2)}) async-start(), calls=%async_computation.19 | async-start | bytes 1310720 | tf_op jit(solution)/shard_map/all_gather | solution.py:203
  52.3 63.7 %copy-start.51 = (f32[512]{0:T(512)}, f32[512]{0:T(512)S(1)}, u32[]{:S(2)}) copy-start(f32[512]{0:T(512)S(1)} %convert_element_type.253) | copy-start | bytes 6148
  114.5 2.9 copy-start.56
  114.5 2.9 copy-start.57
  116.0 21.9 %copy-start.50 = (f32[256]{0:T(256)}, f32[256]{0:T(256)S(1)}, u32[]{:S(2)}) copy-start(f32[256]{0:T(256)S(1)} %broadcast_multiply_fusion.4) | copy-start | bytes 3076
  118.2 51.2 %reduce-scatter.23.cloned.1.call-start = ((), (), s32[]{:S(2)}) async-start(), calls=%async_computation.20 | async-start | bytes 2621440 | tf_op jit(solution)/shard_map/reduce_scatter | solution.py:209
  137.9 50.5 %all-gather.17.cloned.1.call-start = ((), (), s32[]{:S(2)}) async-start(), calls=%async_computation.21 | async-start | bytes 1310720 | tf_op jit(solution)/shard_map/all_gather | solution.py:312
  171.5 57.0 %reduce-scatter.25.cloned.1.call-start = ((), (), s32[]{:S(2)}) async-start(), calls=%async_computation.22 | async-start | bytes 2621440 | tf_op jit(solution)/shard_map/reduce_scatter | solution.py:208
  196.9 50.7 %all-gather.19.cloned.1.call-start = ((), (), s32[]{:S(2)}) async-start(), calls=%async_computation.23 | async-start | bytes 1310720 | tf_op jit(solution)/shard_map/all_gather | solution.py:313
  230.7 51.2 %reduce-scatter.27.cloned.1.call-start = ((), (), s32[]{:S(2)}) async-start(), calls=%async_computation.24 | async-start | bytes 2621440 | tf_op jit(solution)/shard_map/reduce_scatter | solution.py:327
  250.3 55.4 %all-gather.21.cloned.1.call-start = ((), (), s32[]{:S(2)}) async-start(), calls=%async_computation.25 | async-start | bytes 1310720 | tf_op jit(solution)/shard_map/all_gather | solution.py:338
  281.9 5.5 copy-start.11
  288.8 45.3 %all-gather.23.cloned.1.call-start = ((), (), s32[]{:S(2)}) async-start(), calls=%async_computation.26 | async-start | bytes 1310720 | tf_op jit(solution)/shard_map/all_gather | solution.py:339
  289.6 75.1 %reduce-scatter.29.cloned.1.call-start = ((), (), s32[]{:S(2)}) async-start(), calls=%async_computation.27 | async-start | bytes 1310720 | tf_op jit(solution)/shard_map/reduce_scatter | solution.py:359
  314.2 1.8 copy-start.43
  328.2 2.5 copy-start.44
  328.2 3.1 copy-start.24
  329.4 2.5 copy-start.26
  336.9 27.8 %copy-start.49 = (f32[256]{0:T(256)S(1)}, f32[256]{0:T(256)}, u32[]{:S(2)}) copy-start(f32[256]{0:T(256)} %copy-done.48) | copy-start | bytes 3076
  336.9 27.8 %copy-start.53 = (f32[256]{0:T(256)S(1)}, f32[256]{0:T(256)}, u32[]{:S(2)}) copy-start(f32[256]{0:T(256)} %copy-done.52) | copy-start | bytes 3076
  339.6 46.3 %all-gather.9.cloned.1.call-start = ((), (), s32[]{:S(2)}) async-start(), calls=%async_computation.10 | async-start | bytes 1310720 | tf_op jit(solution)/shard_map/all_gather | solution.py:186
  369.0 57.2 %reduce-scatter.11.cloned.1.call-start = ((), (), s32[]{:S(2)}) async-start(), calls=%async_computation.11 | async-start | bytes 2621440 | tf_op jit(solution)/shard_map/reduce_scatter | solution.py:195
  394.6 65.6 %reduce-scatter.13.cloned.1.call-start = ((), (), s32[]{:S(2)}) async-start(), calls=%async_computation.12 | async-start | bytes 2621440 | tf_op jit(solution)/shard_map/reduce_scatter | solution.py:194
  412.5 1.9 copy-start.64
  412.5 1.9 copy-start.66
  412.6 1.9 copy-start.67
  414.4 48.5 %copy-start.68 = (bf16[512]{0:T(512)(128)(2,1)S(1)}, bf16[512]{0:T(512)(128)(2,1)}, u32[]{:S(2)}) copy-start(bf16[512]{0:T(512)(128)(2,1)} %param.44) | copy-start | bytes 3076
  414.4 65.3 %copy-start.21 = (bf16[512,512]{1,0:T(8,128)(2,1)S(1)}, bf16[512,512]{1,0:T(8,128)(2,1)}, u32[]{:S(2)}) copy-start(bf16[512,512]{1,0:T(8,128)(2,1)} %param.43) | copy-start | bytes 1572868
  414.4 65.3 %all-gather.11.cloned.1.call-start = ((), (), s32[]{:S(2)}) async-start(), calls=%async_computation.13 | async-start | bytes 1310720 | tf_op jit(solution)/shard_map/all_gather | solution.py:203
  461.7 22.1 %copy-start.9 = (f32[256,512]{1,0:T(8,128)}, f32[256,512]{1,0:T(8,128)S(1)}, u32[]{:S(2)}) copy-start(f32[256,512]{1,0:T(8,128)S(1)} %get-tuple-element.332) | copy-start | bytes 1572868
  462.8 97.6 %reduce-scatter.17.cloned.1.call-start = ((), (), s32[]{:S(2)}) async-start(), calls=%async_computation.15 | async-start | bytes 2621440 | tf_op jit(solution)/shard_map/reduce_scatter | solution.py:208
  483.8 76.7 %reduce-scatter.15.cloned.1.call-start = ((), (), s32[]{:S(2)}) async-start(), calls=%async_computation.14 | async-start | bytes 2621440 | tf_op jit(solution)/shard_map/reduce_scatter | solution.py:209
  487.4 214.6 %all-reduce.5.cloned.1.call-start = ((), (), s32[]{:S(2)}) async-start(), calls=%async_computation.28 | async-start | bytes 7340032 | tf_op jit(solution)/shard_map/psum | solution.py:386
  487.4 3.4 copy-start.16
  487.4 3.4 copy-start.30
  490.8 2.8 copy-start.13
  492.5 2.1 copy-start.14
  492.5 2.1 copy-start.18
  494.6 3.4 copy-start.20
  499.9 23.4 %copy-start.58 = (f32[512]{0:T(512)S(1)}, f32[512]{0:T(512)}, u32[]{:S(2)}) copy-start(f32[512]{0:T(512)} %get-tuple-element.247) | copy-start | bytes 6148
  499.9 23.4 %copy-start.59 = (f32[512]{0:T(512)S(1)}, f32[512]{0:T(512)}, u32[]{:S(2)}) copy-start(f32[512]{0:T(512)} %get-tuple-element.252) | copy-start | bytes 6148
  499.9 23.4 %copy-start.60 = (f32[512]{0:T(512)S(1)}, f32[512]{0:T(512)}, u32[]{:S(2)}) copy-start(f32[512]{0:T(512)} %get-tuple-element.324) | copy-start | bytes 6148
  499.9 23.4 %copy-start.61 = (f32[512]{0:T(512)S(1)}, f32[512]{0:T(512)}, u32[]{:S(2)}) copy-start(f32[512]{0:T(512)} %get-tuple-element.327) | copy-start | bytes 6148
  499.9 23.4 %copy-start.62 = (f32[512]{0:T(512)S(1)}, f32[512]{0:T(512)}, u32[]{:S(2)}) copy-start(f32[512]{0:T(512)} %get-tuple-element.250) | copy-start | bytes 6148
  499.9 23.4 %copy-start.63 = (f32[512]{0:T(512)S(1)}, f32[512]{0:T(512)}, u32[]{:S(2)}) copy-start(f32[512]{0:T(512)} %get-tuple-element.254) | copy-start | bytes 6148
  499.9 60.5 %copy-start.10 = (f32[256,512]{1,0:T(8,128)S(1)}, f32[256,512]{1,0:T(8,128)}, u32[]{:S(2)}) copy-start(f32[256,512]{1,0:T(8,128)} %copy-done.9) | copy-start | bytes 1572868
  701.9 6.9 copy-start.46
  701.9 7.6 %copy-start.34 = (f32[512,512]{1,0:T(8,128)S(1)}, f32[512,512]{1,0:T(8,128)}, u32[]{:S(2)}) copy-start(f32[512,512]{1,0:T(8,128)} %get-tuple-element.593) | copy-start | bytes 3145732
  703.7 6.8 copy-start.33
  709.5 1.9 copy-start.45
  (41 other events, 43.0 us)
Sparse Core Ops, SparseCore 0:
  13.0 19.4 all-gather.12
  48.9 31.4 reduce-scatter.20
  83.0 31.3 reduce-scatter.18
  118.4 16.7 all-gather.14
  138.0 31.4 reduce-scatter.22
  171.6 16.7 all-gather.16
  197.0 31.4 reduce-scatter.24
  230.8 16.7 all-gather.18
  250.5 31.4 reduce-scatter.26
  289.0 16.7 all-gather.20
  307.9 16.7 all-gather.22
  339.7 24.8 reduce-scatter.28
  369.1 16.7 all-gather.8
  394.7 31.4 reduce-scatter.10
  428.7 31.4 reduce-scatter.12
  462.9 16.7 all-gather.10
  483.9 31.4 reduce-scatter.16
  517.9 31.5 reduce-scatter.14
  555.9 145.9 all-reduce.4
where the time goes:
time: 720 us; the launch traced here: 719 us
  waiting for transfers between devices  464 us (64%)
  matrix products  87.1 us (12%)
  blocking collectives  59.2 us (8%)
  other arithmetic  56.5 us (8%)
  local copies, waits for them, and re-layouts  35.3 us (5%)
  between operations  14.7 us (2%)
    psum x1, waiting for transfers between devices, body(): lax.psum((grad_w_query, grad_b_query, grad_w_key, grad_w_value, grad_b_va...  139 us
    reduce_scatter x2, waiting for transfers between devices, forward_pass(): lax.psum_scatter(matmul(attended, w_out), 'tensor', scatter_dimension=0,...  59.5 us
    reduce_scatter x2, waiting for transfers between devices, forward_pass(): lax.psum_scatter(matmul(gate_rows, gate1_w), 'tensor', scatter_dimension=...  45.8 us
    psum x1, blocking collectives, body(): lax.psum((grad_norm1_gain, grad_norm1_bias, grad_norm2_gain, grad_norm2_b...  37.1 us
    dot_general x15, matrix products, matmul(): return jnp.dot(left, right, preferred_element_type=jnp.float32)  33.9 us
    all_gather x2, waiting for transfers between devices, forward_pass(): lax.all_gather(normed_two_part.astype(jnp.bfloat16), 'tensor', axis=0, ti...  33.6 us
    reduce_scatter x1, waiting for transfers between devices, body(): lax.psum_scatter(normed_two_grad, 'tensor', scatter_dimension=0, tiled=True)  30.8 us
    reduce_scatter x2, waiting for transfers between devices, forward_pass(): lax.psum_scatter(matmul(gate_rows_two, gate2_w), 'tensor', scatter_dimens...  30.8 us
  transfers between devices with their start and end apart: 19, of which 16 were waited for; matrix products, arithmetic and copies ran while one was open for 12% of the time, Pallas kernels for 0%

commit v1 on v0

--- a/solution.py
+++ b/solution.py
@@ -5,6 +5,21 @@
 
 HD = 64
 EPSILON = 1e-05
+
+
+def meet_side(packet):
+    along_axis = "tensor"
+    n_chips = lax.axis_size(along_axis)
+    y2 = list(map(lambda rr: (rr - 1, rr), range(1, n_chips))) + [(n_chips - 1, 0)]
+    local_out = packet
+    samples = [local_out]
+    for _ in range(n_chips - 1):
+        local_out = lax.ppermute(local_out, axis_name=along_axis, perm=y2)
+        samples += [local_out]
+    current_block = jnp.concatenate([*reversed(samples)], axis=0)
+    return jnp.roll(
+        current_block, shift=(lax.axis_index(along_axis) + 1) * local_out.shape[0], axis=0
+    )
 
 
 def matmul(left, right):
@@ -183,7 +198,7 @@
         inputs, norm1_gain.astype(jnp.float32), norm1_bias.astype(jnp.float32)
     )
     normed_low = normed_part.astype(jnp.bfloat16)
-    normed = lax.all_gather(normed_low, "tensor", axis=0, tiled=True)
+    normed = meet_side(normed_low)
     query = (matmul(normed, w_query) + b_query.astype(jnp.float32)).astype(jnp.bfloat16)
     keys = matmul(normed, w_key).astype(jnp.bfloat16)
     values = (matmul(normed, w_value) + b_value.astype(jnp.float32)).astype(jnp.bfloat16)

time: 720 us -> 710 us (0.986)
  local copies, waits for them, and re-layouts: 35.3 us -> 25.2 us
    all_gather x2 -> x0, waiting for transfers between devices: 29.9 us -> none  [forward_pass(): normed = lax.all_gather(normed_low, 'tensor', axis=0, tiled=True)]
    ppermute x0 -> x6, waiting for transfers between devices: none -> 28.5 us  [meet_side(): local_out = lax.ppermute(local_out, axis_name=along_axis, perm=y2)]
    unnamed x133 -> x139, local copies, waits for them, and re-layouts: 18.1 us -> 18.3 us
  transfers between devices with their start and end apart: 19 -> 23, of which waited for: 16 -> 20; matrix products, arithmetic and copies ran while one was open for 12% -> 11% of each run, Pallas kernels for 0% -> 0%
where the time goes in v1:
time: 710 us; the launch traced here: 709 us
  waiting for transfers between devices  470 us (66%)
  matrix products  85.9 us (12%)
  blocking collectives  59.3 us (8%)
  other arithmetic  51.1 us (7%)
  local copies, waits for them, and re-layouts  25.2 us (4%)
  between operations  14.9 us (2%)
    psum x1, waiting for transfers between devices, body(): lax.psum((grad_w_query, grad_b_query, grad_w_key, grad_w_value, grad_b_va...  139 us
    reduce_scatter x2, waiting for transfers between devices, forward_pass(): lax.psum_scatter(matmul(attended, w_out), 'tensor', scatter_dimension=0,...  64.4 us
    reduce_scatter x2, waiting for transfers between devices, forward_pass(): lax.psum_scatter(matmul(gate_rows, gate1_w), 'tensor', scatter_dimension=...  48.9 us
    psum x1, blocking collectives, body(): lax.psum((grad_norm1_gain, grad_norm1_bias, grad_norm2_gain, grad_norm2_b...  37.1 us
    dot_general x15, matrix products, matmul(): return jnp.dot(left, right, preferred_element_type=jnp.float32)  33.7 us
    all_gather x2, waiting for transfers between devices, forward_pass(): lax.all_gather(normed_two_part.astype(jnp.bfloat16), 'tensor', axis=0, ti...  33.6 us
    reduce_scatter x1, waiting for transfers between devices, body(): lax.psum_scatter(normed_two_grad, 'tensor', scatter_dimension=0, tiled=True)  30.8 us
    reduce_scatter x2, waiting for transfers between devices, forward_pass(): lax.psum_scatter(matmul(gate_rows_two, gate2_w), 'tensor', scatter_dimens...  30.8 us
  transfers between devices with their start and end apart: 23, of which 20 were waited for; matrix products, arithmetic and copies ran while one was open for 11% of the time, Pallas kernels for 0%

profile of v1, /device:TPU:0, one launch (start us, length us, event | category | flops | bytes accessed | tf_op | source)
XLA Modules:
  0.0 708.8 jit_solution(18176467662834618916)
XLA Ops:
  12.6 6.0 collective-permute-done.3
  21.9 2.5 collective-permute-done.4
  24.4 1.9 fusion.52
  26.3 3.9 collective-permute-done.5
  32.4 1.7 convolution_convert_fusion.1
  34.2 1.7 fusion.74
  35.9 7.3 %while.38 = (s32[]{:T(128)}, bf16[2,2,512,64]{2,3,1,0:T(8,128)(2,1)S(1)}, f32[2,2,512,1]{2,1,3,0:T(2,128)S(1)}, pred[2,512,1024]{2,1,0:T(8,128)(4,1)S(1)}, bf16[...) while((s32[]{:T(128)}, ...), condition=%wide.region_18.20_spmd, body=%wide.region_15.19_spmd.sunk | while | flops 279977984 | bytes 16171117 | solution.py:116
  43.6 1.8 fusion.151
  45.5 3.0 fusion.128
  48.7 30.3 %reduce-scatter.21.cloned.1.call-done = f32[256,512]{1,0:T(8,128)} async-done(((f32[1024,512]{1,0:T(8,128)}), f32[256,512]{1,0:T(8,128)}) %reduce-scatter.21.cloned.1.call-update) | async-done | bytes 524304 | tf_op jit(solution)/shard_map/reduce_scatter | solution.py:209
  79.0 34.2 %reduce-scatter.19.cloned.1.call-done = f32[256,512]{1,0:T(8,128)} async-done(((f32[1024,512]{1,0:T(8,128)}), f32[256,512]{1,0:T(8,128)}) %reduce-scatter.19.cloned.1.call-update) | async-done | bytes 524304 | tf_op jit(solution)/shard_map/reduce_scatter | solution.py:210
  115.8 16.8 %all-gather.9.cloned.1.call-done = bf16[1024,512]{1,0:T(8,128)(2,1)} async-done(((bf16[256,512]{1,0:T(8,128)(2,1)}), bf16[1024,512]{1,0:T(8,128)(2,1)}) %all-gather.9.cloned.1.call-update) | async-done | bytes 1048592 | tf_op jit(solution)/shard_map/all_gather | solution.py:218
  132.6 2.7 fusion.124
  136.1 30.8 %reduce-scatter.23.cloned.1.call-done = f32[256,512]{1,0:T(8,128)} async-done(((f32[1024,512]{1,0:T(8,128)}), f32[256,512]{1,0:T(8,128)}) %reduce-scatter.23.cloned.1.call-update) | async-done | bytes 524304 | tf_op jit(solution)/shard_map/reduce_scatter | solution.py:224
  166.9 1.9 fusion.103
  170.2 3.4 fusion.152
  173.5 12.2 %all-gather.11.cloned.1.call-done = bf16[1024,512]{1,0:T(8,128)(2,1)} async-done(((bf16[256,512]{1,0:T(8,128)(2,1)}), bf16[1024,512]{1,0:T(8,128)(2,1)}) %all-gather.11.cloned.1.call-update) | async-done | bytes 1048592 | tf_op jit(solution)/shard_map/all_gather | solution.py:327
  185.8 5.5 convert_reduce_fusion.2
  192.3 2.0 fusion.154
  195.7 30.3 %reduce-scatter.25.cloned.1.call-done = f32[256,512]{1,0:T(8,128)} async-done(((f32[1024,512]{1,0:T(8,128)}), f32[256,512]{1,0:T(8,128)}) %reduce-scatter.25.cloned.1.call-update) | async-done | bytes 524304 | tf_op jit(solution)/shard_map/reduce_scatter | solution.py:223
  225.9 2.1 fusion.105
  228.3 3.4 fusion.153
  231.7 13.2 %all-gather.13.cloned.1.call-done = bf16[1024,512]{1,0:T(8,128)(2,1)} async-done(((bf16[256,512]{1,0:T(8,128)(2,1)}), bf16[1024,512]{1,0:T(8,128)(2,1)}) %all-gather.13.cloned.1.call-update) | async-done | bytes 1048592 | tf_op jit(solution)/shard_map/all_gather | solution.py:328
  245.0 2.7 fusion.69
  248.4 30.8 %reduce-scatter.27.cloned.1.call-done = f32[256,512]{1,0:T(8,128)} async-done(((f32[1024,512]{1,0:T(8,128)}), f32[256,512]{1,0:T(8,128)}) %reduce-scatter.27.cloned.1.call-update) | async-done | bytes 524304 | tf_op jit(solution)/shard_map/reduce_scatter | solution.py:342
  279.3 2.0 multiply_reduce_fusion.1
  281.3 3.1 convert_reduce_fusion.6
  286.4 16.2 %all-gather.15.cloned.1.call-done = bf16[1024,512]{1,0:T(8,128)(2,1)} async-done(((bf16[256,512]{1,0:T(8,128)(2,1)}), bf16[1024,512]{1,0:T(8,128)(2,1)}) %all-gather.15.cloned.1.call-update) | async-done | bytes 1048592 | tf_op jit(solution)/shard_map/all_gather | solution.py:353
  302.7 1.7 convolution_convert_fusion
  306.2 14.3 %while.39 = (s32[]{:T(128)}, f32[2,1024,64]{1,2,0:T(8,128)S(1)}, f32[2,1024,64]{1,2,0:T(8,128)}, bf16[2,2,512,64]{2,3,1,0:T(8,128)(2,1)}, pred[2,512,1024]{2,1,0...) while((s32[]{:T(128)}, f32[2,1024,64]{1,2,0:T(8,128)S(1)}, ...), condition=%wide.region_29.31_spmd.clone, body=%wide.region_27.30_spmd.clone.sunk | while | flops 687602688 | bytes 43938064 | solution.py:163
  308.8 1.8 multiply_reduce_fusion.7
  315.9 1.8 multiply_reduce_fusion.7
  323.5 1.8 add_add_fusion
  325.3 2.6 fusion.68
  327.9 2.8 convert_element_type.273
  334.2 21.6 %reduce-scatter.29.cloned.1.call-done = bf16[256,512]{1,0:T(8,128)(2,1)} async-done(((bf16[1024,512]{1,0:T(8,128)(2,1)}), bf16[256,512]{1,0:T(8,128)(2,1)}) %reduce-scatter.29.cloned.1.call-update) | async-done | bytes 262160 | tf_op jit(solution)/shard_map/reduce_scatter | solution.py:374
  355.8 1.9 fusion.108
  357.6 2.2 fusion.96
  359.8 5.8 collective-permute-done
  365.6 5.8 collective-permute-done.1
  372.7 4.5 collective-permute-done.2
  378.7 1.8 fusion.120
  380.5 1.7 fusion.71
  383.2 1.7 copy.43
  385.2 2.4 convolution_convert_fusion.2
  387.6 2.4 fusion.72
  390.0 9.4 %while.37 = (s32[]{:T(128)}, bf16[2,2,512,64]{2,3,1,0:T(8,128)(2,1)S(1)}, pred[2,512,1024]{2,1,0:T(8,128)(4,1)S(1)}, bf16[2,2,512,64]{2,3,1,0:T(8,128)(2,1)}, bf...) while((s32[]{:T(128)}, bf16[2,2,512,64]{2,3,1,0:T(8,128)(2,1)S(1)}, ...), condition=%wide.region_6.8_spmd, body=%wide.region_3.7_spmd.sunk | while | flops 279973888 | bytes 17207420 | solution.py:116
  390.1 2.1 fusion.242
  394.8 2.1 fusion.242
  399.8 1.8 fusion.150
  401.7 14.7 %reduce-scatter.11.cloned.1.call-done = f32[256,512]{1,0:T(8,128)} async-done(((f32[1024,512]{1,0:T(8,128)}), f32[256,512]{1,0:T(8,128)}) %reduce-scatter.11.cloned.1.call-update) | async-done | bytes 524304 | tf_op jit(solution)/shard_map/reduce_scatter | solution.py:210
  416.5 34.1 %reduce-scatter.13.cloned.1.call-done = f32[256,512]{1,0:T(8,128)} async-done(((f32[1024,512]{1,0:T(8,128)}), f32[256,512]{1,0:T(8,128)}) %reduce-scatter.13.cloned.1.call-update) | async-done | bytes 524304 | tf_op jit(solution)/shard_map/reduce_scatter | solution.py:209
  453.2 16.8 %all-gather.7.cloned.1.call-done = bf16[1024,512]{1,0:T(8,128)(2,1)} async-done(((bf16[256,512]{1,0:T(8,128)(2,1)}), bf16[1024,512]{1,0:T(8,128)(2,1)}) %all-gather.7.cloned.1.call-update) | async-done | bytes 1048592 | tf_op jit(solution)/shard_map/all_gather | solution.py:218
  470.0 4.1 fusion.70
  475.0 2.7 fusion.118
  477.8 3.1 fusion.159
  480.9 1.7 fusion.158
  491.4 22.2 %all-reduce.1 = (f32[128]{0:T(128)}, f32[128]{0:T(128)}, f32[512]{0:T(512)}, f32[512]{0:T(512)}, f32[512]{0:T(512)}) all-reduce(f32[128]{0:T(128)S(1)} %reduce_sum.253, f32[128]{0:T(128)S(1)} %reduce_sum.255, f32[512]{0:T(512)S(1)} %copy-done.66, f32[512]{0:T(512)S(1)} %convert_reduce_fusion.1, ...), channel_id=1, replica_groups=mesh['dp'=8,'tensor'=4] {'dp'}, use_global_device_ids=true, to_apply=%region_39.41 | all-reduce | flops 1792 | bytes 14336 | tf_op jit(solution)/shard_map/psum | solution.py:401
  513.6 37.1 %all-reduce = (f32[512]{0:T(512)}, f32[512]{0:T(512)}, f32[512]{0:T(512)}, f32[512]{0:T(512)}, f32[512]{0:T(512)}, /*index=5*/f32[512]{0:T(512)}) all-reduce(f32[512]{0:T(512)S(1)} %copy-done.54, f32[512]{0:T(512)S(1)} %copy-done.55, f32[512]{0:T(512)S(1)} %copy-done.53, ...), channel_id=1, replica_groups=mesh['dp'=8,'tensor'=4] {'dp','tensor'}, use_global_device_ids=true, to_apply=%region_34.36 | all-reduce | flops 3072 | bytes 24576 | tf_op jit(solution)/shard_map/psum | solution.py:381
  550.7 2.3 add_convert_fusion.1
  553.0 139.0 %all-reduce.5.cloned.1.call-done = (f32[512,128]{1,0:T(8,128)}, f32[512,128]{1,0:T(8,128)}, f32[512,128]{1,0:T(8,128)}, f32[128,512]{1,0:T(8,128)}, f32[128,512]...) async-done(((f32[512,128]{1,0:T(8,128)}, f32[512,128]{1,0:T(8,128)}, f32[512,128]{1,0:T(8,128)}, f32[128,512]{1,0:T(8,128)}, ...) | async-done | bytes 3670032 | tf_op jit(solution)/shard_map/psum | solution.py:401
  692.0 1.8 copy.96
  693.8 1.8 copy.97
  697.2 1.7 copy.99
  (316 shorter events, 74.1 us)
Async XLA Ops:
  7.2 178.6 %copy-start = (bf16[512,512]{1,0:T(8,128)(2,1)S(1)}, bf16[512,512]{1,0:T(8,128)(2,1)}, u32[]{:S(2)}) copy-start(bf16[512,512]{1,0:T(8,128)(2,1)} %param.47) | copy-start | bytes 1572868
  7.2 71.8 %reduce-scatter.21.cloned.1.call-start = ((), (), s32[]{:S(2)}) async-start(), calls=%async_computation.16 | async-start | bytes 2621440 | tf_op jit(solution)/shard_map/reduce_scatter | solution.py:209
  8.4 10.2 %copy-start.42 = (f32[256]{0:T(256)}, f32[256]{0:T(256)S(1)}, u32[]{:S(2)}) copy-start(f32[256]{0:T(256)S(1)} %broadcast_multiply_fusion.5) | copy-start | bytes 3076
  9.6 9.0 %copy-start.46 = (f32[256]{0:T(256)}, f32[256]{0:T(256)S(1)}, u32[]{:S(2)}) copy-start(f32[256]{0:T(256)S(1)} %add_rsqrt_fusion.1) | copy-start | bytes 3076
  12.1 6.5 collective-permute-start.3
  18.6 5.8 collective-permute-start.4
  24.4 5.8 collective-permute-start.5
  24.4 7.3 %copy-start.17 = (bf16[512,128]{1,0:T(8,128)(2,1)S(1)}, bf16[512,128]{1,0:T(8,128)(2,1)}, u32[]{:S(2)}) copy-start(bf16[512,128]{1,0:T(8,128)(2,1)} %param.34) | copy-start | bytes 393220
  26.3 6.1 copy-start.23
  31.7 2.4 copy-start.19
  35.9 7.7 %copy-start.21 = (bf16[128,512]{1,0:T(8,128)(2,1)S(1)}, bf16[128,512]{1,0:T(8,128)(2,1)}, u32[]{:S(2)}) copy-start(bf16[128,512]{1,0:T(8,128)(2,1)} %param.39) | copy-start | bytes 393220
  45.4 67.7 %reduce-scatter.19.cloned.1.call-start = ((), (), s32[]{:S(2)}) async-start(), calls=%async_computation.15 | async-start | bytes 2621440 | tf_op jit(solution)/shard_map/reduce_scatter | solution.py:210
  45.5 3.1 copy-start.59
  45.5 3.1 copy-start.57
  45.5 3.1 copy-start.56
  45.5 3.1 copy-start.61
  45.5 67.6 %copy-start.3 = (bf16[256,512]{1,0:T(8,128)(2,1)S(1)}, bf16[256,512]{1,0:T(8,128)(2,1)}, u32[]{:S(2)}) copy-start(bf16[256,512]{1,0:T(8,128)(2,1)} %param.30) | copy-start | bytes 786436
  48.5 84.1 %all-gather.9.cloned.1.call-start = ((), (), s32[]{:S(2)}) async-start(), calls=%async_computation.17 | async-start | bytes 1310720 | tf_op jit(solution)/shard_map/all_gather | solution.py:218
  48.6 66.0 %copy-start.45 = (f32[512]{0:T(512)}, f32[512]{0:T(512)S(1)}, u32[]{:S(2)}) copy-start(f32[512]{0:T(512)S(1)} %convert_element_type.253) | copy-start | bytes 6148
  114.6 20.7 %copy-start.44 = (f32[256]{0:T(256)}, f32[256]{0:T(256)S(1)}, u32[]{:S(2)}) copy-start(f32[256]{0:T(256)S(1)} %broadcast_multiply_fusion.4) | copy-start | bytes 3076
  115.7 51.2 %copy-start.14 = (bf16[256,512]{1,0:T(8,128)(2,1)S(1)}, bf16[256,512]{1,0:T(8,128)(2,1)}, u32[]{:S(2)}) copy-start(bf16[256,512]{1,0:T(8,128)(2,1)} %param.51) | copy-start | bytes 786436
  115.8 51.2 %reduce-scatter.23.cloned.1.call-start = ((), (), s32[]{:S(2)}) async-start(), calls=%async_computation.18 | async-start | bytes 2621440 | tf_op jit(solution)/shard_map/reduce_scatter | solution.py:224
  135.4 50.4 %all-gather.11.cloned.1.call-start = ((), (), s32[]{:S(2)}) async-start(), calls=%async_computation.19 | async-start | bytes 1310720 | tf_op jit(solution)/shard_map/all_gather | solution.py:327
  168.9 57.1 %reduce-scatter.25.cloned.1.call-start = ((), (), s32[]{:S(2)}) async-start(), calls=%async_computation.20 | async-start | bytes 2621440 | tf_op jit(solution)/shard_map/reduce_scatter | solution.py:223
  194.3 50.6 %all-gather.13.cloned.1.call-start = ((), (), s32[]{:S(2)}) async-start(), calls=%async_computation.21 | async-start | bytes 1310720 | tf_op jit(solution)/shard_map/all_gather | solution.py:328
  228.1 51.2 %reduce-scatter.27.cloned.1.call-start = ((), (), s32[]{:S(2)}) async-start(), calls=%async_computation.22 | async-start | bytes 2621440 | tf_op jit(solution)/shard_map/reduce_scatter | solution.py:342
  247.7 55.0 %all-gather.15.cloned.1.call-start = ((), (), s32[]{:S(2)}) async-start(), calls=%async_computation.23 | async-start | bytes 1310720 | tf_op jit(solution)/shard_map/all_gather | solution.py:353
  279.2 5.1 copy-start.6
  285.8 39.5 %all-gather.17.cloned.1.call-start = ((), (), s32[]{:S(2)}) async-start(), calls=%async_computation.24 | async-start | bytes 1310720 | tf_op jit(solution)/shard_map/all_gather | solution.py:354
  286.4 69.4 %reduce-scatter.29.cloned.1.call-start = ((), (), s32[]{:S(2)}) async-start(), calls=%async_computation.25 | async-start | bytes 1310720 | tf_op jit(solution)/shard_map/reduce_scatter | solution.py:374
  320.5 2.1 copy-start.18
  320.6 2.5 copy-start.24
  327.9 27.8 %copy-start.43 = (f32[256]{0:T(256)S(1)}, f32[256]{0:T(256)}, u32[]{:S(2)}) copy-start(f32[256]{0:T(256)} %copy-done.42) | copy-start | bytes 3076
  327.9 27.8 %copy-start.47 = (f32[256]{0:T(256)S(1)}, f32[256]{0:T(256)}, u32[]{:S(2)}) copy-start(f32[256]{0:T(256)} %copy-done.46) | copy-start | bytes 3076
  327.9 29.7 %copy-start.8 = (f32[256,512]{1,0:T(8,128)S(1)}, f32[256,512]{1,0:T(8,128)}, u32[]{:S(2)}) copy-start(f32[256,512]{1,0:T(8,128)} %copy-done.7) | copy-start | bytes 1572868
  330.7 85.7 %reduce-scatter.11.cloned.1.call-start = ((), (), s32[]{:S(2)}) async-start(), calls=%async_computation.10 | async-start | bytes 2621440 | tf_op jit(solution)/shard_map/reduce_scatter | solution.py:210
  359.8 5.8 collective-permute-start
  365.6 5.8 collective-permute-start.1
  371.4 5.8 collective-permute-start.2
  380.5 4.6 copy-start.25
  384.9 65.7 %reduce-scatter.13.cloned.1.call-start = ((), (), s32[]{:S(2)}) async-start(), calls=%async_computation.11 | async-start | bytes 2621440 | tf_op jit(solution)/shard_map/reduce_scatter | solution.py:209
  390.0 9.7 %copy-start.22 = (bf16[128,512]{1,0:T(8,128)(2,1)S(1)}, bf16[128,512]{1,0:T(8,128)(2,1)}, u32[]{:S(2)}) copy-start(bf16[128,512]{1,0:T(8,128)(2,1)} %param.39) | copy-start | bytes 393220
  401.6 51.6 %copy-start.63 = (bf16[512]{0:T(512)(128)(2,1)S(1)}, bf16[512]{0:T(512)(128)(2,1)}, u32[]{:S(2)}) copy-start(bf16[512]{0:T(512)(128)(2,1)} %param.46) | copy-start | bytes 3076
  401.6 68.4 %copy-start.15 = (bf16[512,512]{1,0:T(8,128)(2,1)S(1)}, bf16[512,512]{1,0:T(8,128)(2,1)}, u32[]{:S(2)}) copy-start(bf16[512,512]{1,0:T(8,128)(2,1)} %param.45) | copy-start | bytes 1572868
  401.6 68.4 %all-gather.7.cloned.1.call-start = ((), (), s32[]{:S(2)}) async-start(), calls=%async_computation.12 | async-start | bytes 1310720 | tf_op jit(solution)/shard_map/all_gather | solution.py:218
  453.2 97.6 %reduce-scatter.17.cloned.1.call-start = ((), (), s32[]{:S(2)}) async-start(), calls=%async_computation.14 | async-start | bytes 2621440 | tf_op jit(solution)/shard_map/reduce_scatter | solution.py:223
  474.1 3.7 copy-start.29
  474.1 76.6 %reduce-scatter.15.cloned.1.call-start = ((), (), s32[]{:S(2)}) async-start(), calls=%async_computation.13 | async-start | bytes 2621440 | tf_op jit(solution)/shard_map/reduce_scatter | solution.py:224
  477.8 214.2 %all-reduce.5.cloned.1.call-start = ((), (), s32[]{:S(2)}) async-start(), calls=%async_computation.26 | async-start | bytes 7340032 | tf_op jit(solution)/shard_map/psum | solution.py:401
  477.8 3.1 copy-start.11
  477.8 3.1 copy-start.27
  480.9 2.8 copy-start.2
  483.7 3.5 copy-start.9
  484.9 3.6 copy-start.10
  484.9 3.6 copy-start.13
  490.1 23.4 %copy-start.50 = (f32[512]{0:T(512)S(1)}, f32[512]{0:T(512)}, u32[]{:S(2)}) copy-start(f32[512]{0:T(512)} %get-tuple-element.248) | copy-start | bytes 6148
  490.1 23.4 %copy-start.51 = (f32[512]{0:T(512)S(1)}, f32[512]{0:T(512)}, u32[]{:S(2)}) copy-start(f32[512]{0:T(512)} %get-tuple-element.253) | copy-start | bytes 6148
  490.1 23.4 %copy-start.52 = (f32[512]{0:T(512)S(1)}, f32[512]{0:T(512)}, u32[]{:S(2)}) copy-start(f32[512]{0:T(512)} %get-tuple-element.325) | copy-start | bytes 6148
  490.2 23.4 %copy-start.53 = (f32[512]{0:T(512)S(1)}, f32[512]{0:T(512)}, u32[]{:S(2)}) copy-start(f32[512]{0:T(512)} %get-tuple-element.328) | copy-start | bytes 6148
  490.2 23.4 %copy-start.54 = (f32[512]{0:T(512)S(1)}, f32[512]{0:T(512)}, u32[]{:S(2)}) copy-start(f32[512]{0:T(512)} %get-tuple-element.251) | copy-start | bytes 6148
  490.2 23.4 %copy-start.55 = (f32[512]{0:T(512)S(1)}, f32[512]{0:T(512)}, u32[]{:S(2)}) copy-start(f32[512]{0:T(512)} %get-tuple-element.255) | copy-start | bytes 6148
  692.0 6.9 copy-start.41
  692.0 7.6 %copy-start.32 = (f32[512,512]{1,0:T(8,128)S(1)}, f32[512,512]{1,0:T(8,128)}, u32[]{:S(2)}) copy-start(f32[512,512]{1,0:T(8,128)} %get-tuple-element.594) | copy-start | bytes 3145732
  693.8 6.8 copy-start.31
  (32 other events, 42.2 us)
Sparse Core Ops, SparseCore 0:
  45.5 33.4 reduce-scatter.20
  81.7 31.4 reduce-scatter.18
  115.9 16.7 all-gather.8
  135.5 31.4 reduce-scatter.22
  169.0 16.7 all-gather.10
  194.5 31.4 reduce-scatter.24
  228.2 16.7 all-gather.12
  247.8 31.4 reduce-scatter.26
  285.9 16.7 all-gather.14
  304.7 16.7 all-gather.16
  330.8 24.8 reduce-scatter.28
  385.0 31.4 reduce-scatter.10
  419.1 31.3 reduce-scatter.12
  453.3 16.7 all-gather.6
  474.2 31.4 reduce-scatter.16
  508.2 31.5 reduce-scatter.14
  546.0 145.9 all-reduce.4
